TPU v7x, 1024 devices: a whole 4x4x32 slice. The times are simulated.
1024 devices in a mesh: seq: 64 (over z, core), head: 16 (over y, x).
Axes of the slice: x: 4, y: 4, z: 32, core: 2. Of those that a mesh axis runs over, the one named last changes fastest.
Arguments:
- queries: bfloat16 [8192, 4096], P(('seq', 'head')), as said below
- keys: bfloat16 [8192, 4096], P('seq', 'head'), as said below
- values: bfloat16 [8192, 4096], P('seq', 'head'), may hold values from -6 to 6
- block_order: int32 [64], replicated, may hold values from 0 to 63, each once
Outputs:
- attended: bfloat16 [8192, 4096], P('seq', 'head')
Inputs may be any that keep to these rules, and one draw needn't show every extreme that they name: `block_order`: each storage block holds a different sequence block. `queries`: entries lie within -8 to 8. `keys`: entries lie within -8 to 8.
All inputs are finite; a program needn't handle non-finite values.
Results may differ from a plain program's by a relative error of at most 0.006.
Values may be sent and summed in bfloat16 or wider, within the bound.
A program may use at most 32 MiB of HBM per device.

v0:
```python
import jax
import jax.numpy as jnp
from jax import lax
from jax.sharding import PartitionSpec as P

HEAD_DIM = 128


def shifted(block, axis, distance):
    devices = range(lax.axis_size(axis))
    route = [((i - distance) % len(devices), i) for i in devices]
    return lax.ppermute(block, axis, route)


def body(queries, keys, values, block_order):
    seq_count = lax.axis_size("seq")
    me_index = lax.axis_index("seq")
    local_q = lax.all_to_all(queries, "head", split_axis=1, concat_axis=0, tiled=True)
    rows = local_q.shape[0]
    head_count = local_q.shape[1] // HEAD_DIM
    q_three = local_q.reshape(rows, head_count, HEAD_DIM)
    mine = block_order[me_index]
    scale = 1.0 / HEAD_DIM**0.5

    def tile(state, kv_pair, allowed):
        rowmax, total, accum = state
        key_count = kv_pair[0].shape[0]
        k_three = kv_pair[0].reshape(key_count, head_count, HEAD_DIM)
        v_three = kv_pair[1].reshape(key_count, head_count, HEAD_DIM)
        scores = (
            jnp.einsum("qhd,khd->hqk", q_three, k_three, preferred_element_type=jnp.float32) * scale
        )
        scores = jnp.where(allowed[None], scores, jnp.float32(-1e30))
        new_max = jnp.maximum(rowmax, jnp.max(scores, axis=2))
        factor = jnp.exp(rowmax - new_max)
        weight = jnp.where(allowed[None], jnp.exp(scores - new_max[:, :, None]), jnp.float32(0.0))
        total = total * factor + jnp.sum(weight, axis=2)
        mixed = jnp.einsum(
            "hqk,khd->qhd", weight.astype(jnp.bfloat16), v_three, preferred_element_type=jnp.float32
        )
        accum = accum * jnp.transpose(factor)[:, :, None] + mixed
        return (new_max, total, accum)

    def absorb(state, kv_pair, source):
        visible = block_order[source % seq_count] < mine
        allowed = jnp.broadcast_to(visible, (rows, rows))
        return tile(state, kv_pair, allowed)

    start_state = (
        jnp.full((head_count, rows), -1e30, jnp.float32),
        jnp.zeros((head_count, rows), jnp.float32),
        jnp.zeros((rows, head_count, HEAD_DIM), jnp.float32),
    )
    query_idx = lax.broadcasted_iota(jnp.int32, (rows, rows), 0)
    key_idx = lax.broadcasted_iota(jnp.int32, (rows, rows), 1)
    state = tile(start_state, (keys, values), key_idx <= query_idx)

    def cycle_turn(step, carry):
        kv_pair, st = carry
        kv_pair = shifted((kv_pair[0], kv_pair[1]), "seq", 1)
        st = absorb(st, kv_pair, me_index - step + seq_count)
        return (kv_pair, st)

    kv_last, state = lax.fori_loop(1, seq_count, cycle_turn, ((keys, values), state))
    rowmax, total, accum = state
    result = accum / jnp.transpose(total)[:, :, None]
    return result.reshape(rows, head_count * HEAD_DIM).astype(jnp.bfloat16)


def solution(mesh):
    in_specs = (P(("seq", "head"), None), P("seq", "head"), P("seq", "head"), P())
    out_specs = P("seq", "head")
    return jax.shard_map(body, mesh=mesh, in_specs=in_specs, out_specs=out_specs, check_vma=False)
```

profile of v0, /device:TPU:1, one launch (start us, length us, event | category | flops | bytes accessed | tf_op | source)
XLA Modules:
  0.0 397.0 jit_solution(235645686229912692)
XLA Ops:
  0.0 7.7 %all-to-all-start = ((bf16[8,16,256]{2,0,1:T(8,128)(2,1)}), bf16[8,16,256]{2,0,1:T(8,128)(2,1)S(1)}, u32[]{:S(2)}, u32[]{:S(2)}) async-start(bf16[8,16,256]{2,0,1:T(8,128)(2,1)} %bitcast.62), calls=%async_computation | async-start | bytes 131072 | tf_op jit(solution)/shard_map/all_to_all | solution.py:18
  10.0 4.3 %all-to-all-done = bf16[8,16,256]{2,0,1:T(8,128)(2,1)S(1)} async-done(((bf16[8,16,256]{2,0,1:T(8,128)(2,1)}), bf16[8,16,256]{2,0,1:T(8,128)(2,1)S(1)}, u32[]{:S(2)}, u32[]{:S(2)}) %all-to-all-start) | async-done | bytes 65568 | tf_op jit(solution)/shard_map/all_to_all | solution.py:18
  14.8 381.5 %while.23 = (s32[]{:T(128)}, bf16[128,256]{0,1:T(8,128)(2,1)S(1)}, bf16[128,256]{0,1:T(8,128)(2,1)S(1)}, f32[2,128]{1,0:T(2,128)S(1)}, f32[2,128]{1,0:T(2,128)S(...) while((s32[]{:T(128)}, bf16[128,256]{0,1:T(8,128)(2,1)S(1)}, ...), condition=%wide.region_5.6_spmd, body=%wide.region_2.5_spmd.sunk | while | flops 17138452 | bytes 1655188 | solution.py:64
  14.8 3.6 collective-permute-start
  20.4 6.3 %collective-permute-done = bf16[128,256]{0,1:T(8,128)(2,1)S(1)} collective-permute-done((bf16[128,256]{0,1:T(8,128)(2,1)S(1)}, bf16[128,256]{0,1:T(8,128)(2,1)S(1)}, u32[]{:S(2)}, u32[]{:S(2)}) %collective-permute-start) | collective-permute-done | bytes 65568 | tf_op jit(solution)/shard_map/while/body/eval_jaxpr/ppermute | solution.py:12
  29.3 6.1 %collective-permute-done = bf16[128,256]{0,1:T(8,128)(2,1)S(1)} collective-permute-done((bf16[128,256]{0,1:T(8,128)(2,1)S(1)}, bf16[128,256]{0,1:T(8,128)(2,1)S(1)}, u32[]{:S(2)}, u32[]{:S(2)}) %collective-permute-start) | collective-permute-done | bytes 65568 | tf_op jit(solution)/shard_map/while/body/eval_jaxpr/ppermute | solution.py:12
  38.0 3.3 collective-permute-done
  43.9 3.3 collective-permute-done
  49.8 3.3 collective-permute-done
  55.7 3.3 collective-permute-done
  61.6 3.3 collective-permute-done
  67.5 3.3 collective-permute-done
  73.4 3.3 collective-permute-done
  79.3 3.3 collective-permute-done
  85.2 3.3 collective-permute-done
  91.2 3.3 collective-permute-done
  97.1 3.3 collective-permute-done
  103.0 3.3 collective-permute-done
  108.9 3.3 collective-permute-done
  114.8 3.3 collective-permute-done
  120.7 3.3 collective-permute-done
  126.6 3.3 collective-permute-done
  132.5 3.3 collective-permute-done
  138.4 3.3 collective-permute-done
  144.3 3.3 collective-permute-done
  150.2 3.3 collective-permute-done
  156.1 3.3 collective-permute-done
  162.0 3.3 collective-permute-done
  167.9 3.3 collective-permute-done
  173.8 3.3 collective-permute-done
  179.7 3.3 collective-permute-done
  185.6 3.3 collective-permute-done
  191.6 3.3 collective-permute-done
  197.5 3.3 collective-permute-done
  203.4 3.3 collective-permute-done
  209.3 3.3 collective-permute-done
  215.2 3.3 collective-permute-done
  221.1 3.3 collective-permute-done
  227.0 3.3 collective-permute-done
  232.9 3.3 collective-permute-done
  238.8 3.3 collective-permute-done
  244.7 3.3 collective-permute-done
  250.6 3.3 collective-permute-done
  256.5 3.3 collective-permute-done
  262.4 3.3 collective-permute-done
  268.3 3.3 collective-permute-done
  274.2 3.3 collective-permute-done
  280.1 3.3 collective-permute-done
  286.0 3.3 collective-permute-done
  292.0 3.3 collective-permute-done
  303.8 3.3 collective-permute-done
  309.7 3.3 collective-permute-done
  315.6 3.3 collective-permute-done
  321.5 3.3 collective-permute-done
  327.4 3.3 collective-permute-done
  333.3 3.3 collective-permute-done
  339.2 3.3 collective-permute-done
  345.1 3.3 collective-permute-done
  356.9 3.3 collective-permute-done
  362.8 3.3 collective-permute-done
  374.6 3.3 collective-permute-done
  380.5 3.3 collective-permute-done
  386.5 3.3 collective-permute-done
  392.4 3.3 collective-permute-done
  (776 shorter events, 92.2 us)
Async XLA Ops:
  0.0 14.2 %all-to-all-start = ((bf16[8,16,256]{2,0,1:T(8,128)(2,1)}), bf16[8,16,256]{2,0,1:T(8,128)(2,1)S(1)}, u32[]{:S(2)}, u32[]{:S(2)}) async-start(bf16[8,16,256]{2,0,1:T(8,128)(2,1)} %bitcast.62), calls=%async_computation | async-start | bytes 131072 | tf_op jit(solution)/shard_map/all_to_all | solution.py:18
  14.8 11.9 %collective-permute-start = (bf16[128,256]{0,1:T(8,128)(2,1)S(1)}, bf16[128,256]{0,1:T(8,128)(2,1)S(1)}, u32[]{:S(2)}, u32[]{:S(2)}) collective-permute-start(bf16[128,256]{0,1:T(8,128)(2,1)S(1)} %get-tuple-element.373), channel_id=1, source_target_pairs={{1008,0},{0,16},{16,32},{32,48},{48,64},{64,80},{80,96},{96,112},{... | collective-permute-start | bytes 196616 | tf_op jit(solution)/shard_map/while/body/eval_jaxpr/ppermute | solution.py:12
  18.4 8.6 %collective-permute-start.1 = (bf16[128,256]{0,1:T(8,128)(2,1)S(1)}, bf16[128,256]{0,1:T(8,128)(2,1)S(1)}, u32[]{:S(2)}, u32[]{:S(2)}) collective-permute-start(bf16[128,256]{0,1:T(8,128)(2,1)S(1)} %get-tuple-element.374), channel_id=1, source_target_pairs={{1008,0},{0,16},{16,32},{32,48},{48,64},{64,80},{80,96},{96,112},{... | collective-permute-start | bytes 196616 | tf_op jit(solution)/shard_map/while/body/eval_jaxpr/ppermute | solution.py:12
  27.3 8.1 %collective-permute-start = (bf16[128,256]{0,1:T(8,128)(2,1)S(1)}, bf16[128,256]{0,1:T(8,128)(2,1)S(1)}, u32[]{:S(2)}, u32[]{:S(2)}) collective-permute-start(bf16[128,256]{0,1:T(8,128)(2,1)S(1)} %get-tuple-element.373), channel_id=1, source_target_pairs={{1008,0},{0,16},{16,32},{32,48},{48,64},{64,80},{80,96},{96,112},{... | collective-permute-start | bytes 196616 | tf_op jit(solution)/shard_map/while/body/eval_jaxpr/ppermute | solution.py:12
  27.3 8.4 %collective-permute-start.1 = (bf16[128,256]{0,1:T(8,128)(2,1)S(1)}, bf16[128,256]{0,1:T(8,128)(2,1)S(1)}, u32[]{:S(2)}, u32[]{:S(2)}) collective-permute-start(bf16[128,256]{0,1:T(8,128)(2,1)S(1)} %get-tuple-element.374), channel_id=1, source_target_pairs={{1008,0},{0,16},{16,32},{32,48},{48,64},{64,80},{80,96},{96,112},{... | collective-permute-start | bytes 196616 | tf_op jit(solution)/shard_map/while/body/eval_jaxpr/ppermute | solution.py:12
  36.0 5.6 %collective-permute-start.1 = (bf16[128,256]{0,1:T(8,128)(2,1)S(1)}, bf16[128,256]{0,1:T(8,128)(2,1)S(1)}, u32[]{:S(2)}, u32[]{:S(2)}) collective-permute-start(bf16[128,256]{0,1:T(8,128)(2,1)S(1)} %get-tuple-element.374), channel_id=1, source_target_pairs={{1008,0},{0,16},{16,32},{32,48},{48,64},{64,80},{80,96},{96,112},{... | collective-permute-start | bytes 196616 | tf_op jit(solution)/shard_map/while/body/eval_jaxpr/ppermute | solution.py:12
  41.9 5.6 %collective-permute-start.1 = (bf16[128,256]{0,1:T(8,128)(2,1)S(1)}, bf16[128,256]{0,1:T(8,128)(2,1)S(1)}, u32[]{:S(2)}, u32[]{:S(2)}) collective-permute-start(bf16[128,256]{0,1:T(8,128)(2,1)S(1)} %get-tuple-element.374), channel_id=1, source_target_pairs={{1008,0},{0,16},{16,32},{32,48},{48,64},{64,80},{80,96},{96,112},{... | collective-permute-start | bytes 196616 | tf_op jit(solution)/shard_map/while/body/eval_jaxpr/ppermute | solution.py:12
  47.8 5.6 %collective-permute-start.1 = (bf16[128,256]{0,1:T(8,128)(2,1)S(1)}, bf16[128,256]{0,1:T(8,128)(2,1)S(1)}, u32[]{:S(2)}, u32[]{:S(2)}) collective-permute-start(bf16[128,256]{0,1:T(8,128)(2,1)S(1)} %get-tuple-element.374), channel_id=1, source_target_pairs={{1008,0},{0,16},{16,32},{32,48},{48,64},{64,80},{80,96},{96,112},{... | collective-permute-start | bytes 196616 | tf_op jit(solution)/shard_map/while/body/eval_jaxpr/ppermute | solution.py:12
  53.7 5.6 %collective-permute-start.1 = (bf16[128,256]{0,1:T(8,128)(2,1)S(1)}, bf16[128,256]{0,1:T(8,128)(2,1)S(1)}, u32[]{:S(2)}, u32[]{:S(2)}) collective-permute-start(bf16[128,256]{0,1:T(8,128)(2,1)S(1)} %get-tuple-element.374), channel_id=1, source_target_pairs={{1008,0},{0,16},{16,32},{32,48},{48,64},{64,80},{80,96},{96,112},{... | collective-permute-start | bytes 196616 | tf_op jit(solution)/shard_map/while/body/eval_jaxpr/ppermute | solution.py:12
  59.6 5.6 %collective-permute-start.1 = (bf16[128,256]{0,1:T(8,128)(2,1)S(1)}, bf16[128,256]{0,1:T(8,128)(2,1)S(1)}, u32[]{:S(2)}, u32[]{:S(2)}) collective-permute-start(bf16[128,256]{0,1:T(8,128)(2,1)S(1)} %get-tuple-element.374), channel_id=1, source_target_pairs={{1008,0},{0,16},{16,32},{32,48},{48,64},{64,80},{80,96},{96,112},{... | collective-permute-start | bytes 196616 | tf_op jit(solution)/shard_map/while/body/eval_jaxpr/ppermute | solution.py:12
  65.6 5.6 %collective-permute-start.1 = (bf16[128,256]{0,1:T(8,128)(2,1)S(1)}, bf16[128,256]{0,1:T(8,128)(2,1)S(1)}, u32[]{:S(2)}, u32[]{:S(2)}) collective-permute-start(bf16[128,256]{0,1:T(8,128)(2,1)S(1)} %get-tuple-element.374), channel_id=1, source_target_pairs={{1008,0},{0,16},{16,32},{32,48},{48,64},{64,80},{80,96},{96,112},{... | collective-permute-start | bytes 196616 | tf_op jit(solution)/shard_map/while/body/eval_jaxpr/ppermute | solution.py:12
  71.5 5.6 %collective-permute-start.1 = (bf16[128,256]{0,1:T(8,128)(2,1)S(1)}, bf16[128,256]{0,1:T(8,128)(2,1)S(1)}, u32[]{:S(2)}, u32[]{:S(2)}) collective-permute-start(bf16[128,256]{0,1:T(8,128)(2,1)S(1)} %get-tuple-element.374), channel_id=1, source_target_pairs={{1008,0},{0,16},{16,32},{32,48},{48,64},{64,80},{80,96},{96,112},{... | collective-permute-start | bytes 196616 | tf_op jit(solution)/shard_map/while/body/eval_jaxpr/ppermute | solution.py:12
  77.4 5.6 %collective-permute-start.1 = (bf16[128,256]{0,1:T(8,128)(2,1)S(1)}, bf16[128,256]{0,1:T(8,128)(2,1)S(1)}, u32[]{:S(2)}, u32[]{:S(2)}) collective-permute-start(bf16[128,256]{0,1:T(8,128)(2,1)S(1)} %get-tuple-element.374), channel_id=1, source_target_pairs={{1008,0},{0,16},{16,32},{32,48},{48,64},{64,80},{80,96},{96,112},{... | collective-permute-start | bytes 196616 | tf_op jit(solution)/shard_map/while/body/eval_jaxpr/ppermute | solution.py:12
  83.3 5.6 %collective-permute-start.1 = (bf16[128,256]{0,1:T(8,128)(2,1)S(1)}, bf16[128,256]{0,1:T(8,128)(2,1)S(1)}, u32[]{:S(2)}, u32[]{:S(2)}) collective-permute-start(bf16[128,256]{0,1:T(8,128)(2,1)S(1)} %get-tuple-element.374), channel_id=1, source_target_pairs={{1008,0},{0,16},{16,32},{32,48},{48,64},{64,80},{80,96},{96,112},{... | collective-permute-start | bytes 196616 | tf_op jit(solution)/shard_map/while/body/eval_jaxpr/ppermute | solution.py:12
  89.2 5.6 %collective-permute-start.1 = (bf16[128,256]{0,1:T(8,128)(2,1)S(1)}, bf16[128,256]{0,1:T(8,128)(2,1)S(1)}, u32[]{:S(2)}, u32[]{:S(2)}) collective-permute-start(bf16[128,256]{0,1:T(8,128)(2,1)S(1)} %get-tuple-element.374), channel_id=1, source_target_pairs={{1008,0},{0,16},{16,32},{32,48},{48,64},{64,80},{80,96},{96,112},{... | collective-permute-start | bytes 196616 | tf_op jit(solution)/shard_map/while/body/eval_jaxpr/ppermute | solution.py:12
  95.1 5.6 %collective-permute-start.1 = (bf16[128,256]{0,1:T(8,128)(2,1)S(1)}, bf16[128,256]{0,1:T(8,128)(2,1)S(1)}, u32[]{:S(2)}, u32[]{:S(2)}) collective-permute-start(bf16[128,256]{0,1:T(8,128)(2,1)S(1)} %get-tuple-element.374), channel_id=1, source_target_pairs={{1008,0},{0,16},{16,32},{32,48},{48,64},{64,80},{80,96},{96,112},{... | collective-permute-start | bytes 196616 | tf_op jit(solution)/shard_map/while/body/eval_jaxpr/ppermute | solution.py:12
  101.0 5.6 %collective-permute-start.1 = (bf16[128,256]{0,1:T(8,128)(2,1)S(1)}, bf16[128,256]{0,1:T(8,128)(2,1)S(1)}, u32[]{:S(2)}, u32[]{:S(2)}) collective-permute-start(bf16[128,256]{0,1:T(8,128)(2,1)S(1)} %get-tuple-element.374), channel_id=1, source_target_pairs={{1008,0},{0,16},{16,32},{32,48},{48,64},{64,80},{80,96},{96,112},{... | collective-permute-start | bytes 196616 | tf_op jit(solution)/shard_map/while/body/eval_jaxpr/ppermute | solution.py:12
  106.9 5.6 %collective-permute-start.1 = (bf16[128,256]{0,1:T(8,128)(2,1)S(1)}, bf16[128,256]{0,1:T(8,128)(2,1)S(1)}, u32[]{:S(2)}, u32[]{:S(2)}) collective-permute-start(bf16[128,256]{0,1:T(8,128)(2,1)S(1)} %get-tuple-element.374), channel_id=1, source_target_pairs={{1008,0},{0,16},{16,32},{32,48},{48,64},{64,80},{80,96},{96,112},{... | collective-permute-start | bytes 196616 | tf_op jit(solution)/shard_map/while/body/eval_jaxpr/ppermute | solution.py:12
  112.8 5.6 %collective-permute-start.1 = (bf16[128,256]{0,1:T(8,128)(2,1)S(1)}, bf16[128,256]{0,1:T(8,128)(2,1)S(1)}, u32[]{:S(2)}, u32[]{:S(2)}) collective-permute-start(bf16[128,256]{0,1:T(8,128)(2,1)S(1)} %get-tuple-element.374), channel_id=1, source_target_pairs={{1008,0},{0,16},{16,32},{32,48},{48,64},{64,80},{80,96},{96,112},{... | collective-permute-start | bytes 196616 | tf_op jit(solution)/shard_map/while/body/eval_jaxpr/ppermute | solution.py:12
  118.7 5.6 %collective-permute-start.1 = (bf16[128,256]{0,1:T(8,128)(2,1)S(1)}, bf16[128,256]{0,1:T(8,128)(2,1)S(1)}, u32[]{:S(2)}, u32[]{:S(2)}) collective-permute-start(bf16[128,256]{0,1:T(8,128)(2,1)S(1)} %get-tuple-element.374), channel_id=1, source_target_pairs={{1008,0},{0,16},{16,32},{32,48},{48,64},{64,80},{80,96},{96,112},{... | collective-permute-start | bytes 196616 | tf_op jit(solution)/shard_map/while/body/eval_jaxpr/ppermute | solution.py:12
  124.6 5.6 %collective-permute-start.1 = (bf16[128,256]{0,1:T(8,128)(2,1)S(1)}, bf16[128,256]{0,1:T(8,128)(2,1)S(1)}, u32[]{:S(2)}, u32[]{:S(2)}) collective-permute-start(bf16[128,256]{0,1:T(8,128)(2,1)S(1)} %get-tuple-element.374), channel_id=1, source_target_pairs={{1008,0},{0,16},{16,32},{32,48},{48,64},{64,80},{80,96},{96,112},{... | collective-permute-start | bytes 196616 | tf_op jit(solution)/shard_map/while/body/eval_jaxpr/ppermute | solution.py:12
  130.5 5.6 %collective-permute-start.1 = (bf16[128,256]{0,1:T(8,128)(2,1)S(1)}, bf16[128,256]{0,1:T(8,128)(2,1)S(1)}, u32[]{:S(2)}, u32[]{:S(2)}) collective-permute-start(bf16[128,256]{0,1:T(8,128)(2,1)S(1)} %get-tuple-element.374), channel_id=1, source_target_pairs={{1008,0},{0,16},{16,32},{32,48},{48,64},{64,80},{80,96},{96,112},{... | collective-permute-start | bytes 196616 | tf_op jit(solution)/shard_map/while/body/eval_jaxpr/ppermute | solution.py:12
  136.4 5.6 %collective-permute-start.1 = (bf16[128,256]{0,1:T(8,128)(2,1)S(1)}, bf16[128,256]{0,1:T(8,128)(2,1)S(1)}, u32[]{:S(2)}, u32[]{:S(2)}) collective-permute-start(bf16[128,256]{0,1:T(8,128)(2,1)S(1)} %get-tuple-element.374), channel_id=1, source_target_pairs={{1008,0},{0,16},{16,32},{32,48},{48,64},{64,80},{80,96},{96,112},{... | collective-permute-start | bytes 196616 | tf_op jit(solution)/shard_map/while/body/eval_jaxpr/ppermute | solution.py:12
  142.3 5.6 %collective-permute-start.1 = (bf16[128,256]{0,1:T(8,128)(2,1)S(1)}, bf16[128,256]{0,1:T(8,128)(2,1)S(1)}, u32[]{:S(2)}, u32[]{:S(2)}) collective-permute-start(bf16[128,256]{0,1:T(8,128)(2,1)S(1)} %get-tuple-element.374), channel_id=1, source_target_pairs={{1008,0},{0,16},{16,32},{32,48},{48,64},{64,80},{80,96},{96,112},{... | collective-permute-start | bytes 196616 | tf_op jit(solution)/shard_map/while/body/eval_jaxpr/ppermute | solution.py:12
  148.2 5.6 %collective-permute-start.1 = (bf16[128,256]{0,1:T(8,128)(2,1)S(1)}, bf16[128,256]{0,1:T(8,128)(2,1)S(1)}, u32[]{:S(2)}, u32[]{:S(2)}) collective-permute-start(bf16[128,256]{0,1:T(8,128)(2,1)S(1)} %get-tuple-element.374), channel_id=1, source_target_pairs={{1008,0},{0,16},{16,32},{32,48},{48,64},{64,80},{80,96},{96,112},{... | collective-permute-start | bytes 196616 | tf_op jit(solution)/shard_map/while/body/eval_jaxpr/ppermute | solution.py:12
  154.1 5.6 %collective-permute-start.1 = (bf16[128,256]{0,1:T(8,128)(2,1)S(1)}, bf16[128,256]{0,1:T(8,128)(2,1)S(1)}, u32[]{:S(2)}, u32[]{:S(2)}) collective-permute-start(bf16[128,256]{0,1:T(8,128)(2,1)S(1)} %get-tuple-element.374), channel_id=1, source_target_pairs={{1008,0},{0,16},{16,32},{32,48},{48,64},{64,80},{80,96},{96,112},{... | collective-permute-start | bytes 196616 | tf_op jit(solution)/shard_map/while/body/eval_jaxpr/ppermute | solution.py:12
  160.1 5.6 %collective-permute-start.1 = (bf16[128,256]{0,1:T(8,128)(2,1)S(1)}, bf16[128,256]{0,1:T(8,128)(2,1)S(1)}, u32[]{:S(2)}, u32[]{:S(2)}) collective-permute-start(bf16[128,256]{0,1:T(8,128)(2,1)S(1)} %get-tuple-element.374), channel_id=1, source_target_pairs={{1008,0},{0,16},{16,32},{32,48},{48,64},{64,80},{80,96},{96,112},{... | collective-permute-start | bytes 196616 | tf_op jit(solution)/shard_map/while/body/eval_jaxpr/ppermute | solution.py:12
  166.0 5.6 %collective-permute-start.1 = (bf16[128,256]{0,1:T(8,128)(2,1)S(1)}, bf16[128,256]{0,1:T(8,128)(2,1)S(1)}, u32[]{:S(2)}, u32[]{:S(2)}) collective-permute-start(bf16[128,256]{0,1:T(8,128)(2,1)S(1)} %get-tuple-element.374), channel_id=1, source_target_pairs={{1008,0},{0,16},{16,32},{32,48},{48,64},{64,80},{80,96},{96,112},{... | collective-permute-start | bytes 196616 | tf_op jit(solution)/shard_map/while/body/eval_jaxpr/ppermute | solution.py:12
  171.9 5.6 %collective-permute-start.1 = (bf16[128,256]{0,1:T(8,128)(2,1)S(1)}, bf16[128,256]{0,1:T(8,128)(2,1)S(1)}, u32[]{:S(2)}, u32[]{:S(2)}) collective-permute-start(bf16[128,256]{0,1:T(8,128)(2,1)S(1)} %get-tuple-element.374), channel_id=1, source_target_pairs={{1008,0},{0,16},{16,32},{32,48},{48,64},{64,80},{80,96},{96,112},{... | collective-permute-start | bytes 196616 | tf_op jit(solution)/shard_map/while/body/eval_jaxpr/ppermute | solution.py:12
  177.8 5.6 %collective-permute-start.1 = (bf16[128,256]{0,1:T(8,128)(2,1)S(1)}, bf16[128,256]{0,1:T(8,128)(2,1)S(1)}, u32[]{:S(2)}, u32[]{:S(2)}) collective-permute-start(bf16[128,256]{0,1:T(8,128)(2,1)S(1)} %get-tuple-element.374), channel_id=1, source_target_pairs={{1008,0},{0,16},{16,32},{32,48},{48,64},{64,80},{80,96},{96,112},{... | collective-permute-start | bytes 196616 | tf_op jit(solution)/shard_map/while/body/eval_jaxpr/ppermute | solution.py:12
  183.7 5.6 %collective-permute-start.1 = (bf16[128,256]{0,1:T(8,128)(2,1)S(1)}, bf16[128,256]{0,1:T(8,128)(2,1)S(1)}, u32[]{:S(2)}, u32[]{:S(2)}) collective-permute-start(bf16[128,256]{0,1:T(8,128)(2,1)S(1)} %get-tuple-element.374), channel_id=1, source_target_pairs={{1008,0},{0,16},{16,32},{32,48},{48,64},{64,80},{80,96},{96,112},{... | collective-permute-start | bytes 196616 | tf_op jit(solution)/shard_map/while/body/eval_jaxpr/ppermute | solution.py:12
  189.6 5.6 %collective-permute-start.1 = (bf16[128,256]{0,1:T(8,128)(2,1)S(1)}, bf16[128,256]{0,1:T(8,128)(2,1)S(1)}, u32[]{:S(2)}, u32[]{:S(2)}) collective-permute-start(bf16[128,256]{0,1:T(8,128)(2,1)S(1)} %get-tuple-element.374), channel_id=1, source_target_pairs={{1008,0},{0,16},{16,32},{32,48},{48,64},{64,80},{80,96},{96,112},{... | collective-permute-start | bytes 196616 | tf_op jit(solution)/shard_map/while/body/eval_jaxpr/ppermute | solution.py:12
  195.5 5.6 %collective-permute-start.1 = (bf16[128,256]{0,1:T(8,128)(2,1)S(1)}, bf16[128,256]{0,1:T(8,128)(2,1)S(1)}, u32[]{:S(2)}, u32[]{:S(2)}) collective-permute-start(bf16[128,256]{0,1:T(8,128)(2,1)S(1)} %get-tuple-element.374), channel_id=1, source_target_pairs={{1008,0},{0,16},{16,32},{32,48},{48,64},{64,80},{80,96},{96,112},{... | collective-permute-start | bytes 196616 | tf_op jit(solution)/shard_map/while/body/eval_jaxpr/ppermute | solution.py:12
  201.4 5.6 %collective-permute-start.1 = (bf16[128,256]{0,1:T(8,128)(2,1)S(1)}, bf16[128,256]{0,1:T(8,128)(2,1)S(1)}, u32[]{:S(2)}, u32[]{:S(2)}) collective-permute-start(bf16[128,256]{0,1:T(8,128)(2,1)S(1)} %get-tuple-element.374), channel_id=1, source_target_pairs={{1008,0},{0,16},{16,32},{32,48},{48,64},{64,80},{80,96},{96,112},{... | collective-permute-start | bytes 196616 | tf_op jit(solution)/shard_map/while/body/eval_jaxpr/ppermute | solution.py:12
  207.3 5.6 %collective-permute-start.1 = (bf16[128,256]{0,1:T(8,128)(2,1)S(1)}, bf16[128,256]{0,1:T(8,128)(2,1)S(1)}, u32[]{:S(2)}, u32[]{:S(2)}) collective-permute-start(bf16[128,256]{0,1:T(8,128)(2,1)S(1)} %get-tuple-element.374), channel_id=1, source_target_pairs={{1008,0},{0,16},{16,32},{32,48},{48,64},{64,80},{80,96},{96,112},{... | collective-permute-start | bytes 196616 | tf_op jit(solution)/shard_map/while/body/eval_jaxpr/ppermute | solution.py:12
  213.2 5.6 %collective-permute-start.1 = (bf16[128,256]{0,1:T(8,128)(2,1)S(1)}, bf16[128,256]{0,1:T(8,128)(2,1)S(1)}, u32[]{:S(2)}, u32[]{:S(2)}) collective-permute-start(bf16[128,256]{0,1:T(8,128)(2,1)S(1)} %get-tuple-element.374), channel_id=1, source_target_pairs={{1008,0},{0,16},{16,32},{32,48},{48,64},{64,80},{80,96},{96,112},{... | collective-permute-start | bytes 196616 | tf_op jit(solution)/shard_map/while/body/eval_jaxpr/ppermute | solution.py:12
  219.1 5.6 %collective-permute-start.1 = (bf16[128,256]{0,1:T(8,128)(2,1)S(1)}, bf16[128,256]{0,1:T(8,128)(2,1)S(1)}, u32[]{:S(2)}, u32[]{:S(2)}) collective-permute-start(bf16[128,256]{0,1:T(8,128)(2,1)S(1)} %get-tuple-element.374), channel_id=1, source_target_pairs={{1008,0},{0,16},{16,32},{32,48},{48,64},{64,80},{80,96},{96,112},{... | collective-permute-start | bytes 196616 | tf_op jit(solution)/shard_map/while/body/eval_jaxpr/ppermute | solution.py:12
  225.0 5.6 %collective-permute-start.1 = (bf16[128,256]{0,1:T(8,128)(2,1)S(1)}, bf16[128,256]{0,1:T(8,128)(2,1)S(1)}, u32[]{:S(2)}, u32[]{:S(2)}) collective-permute-start(bf16[128,256]{0,1:T(8,128)(2,1)S(1)} %get-tuple-element.374), channel_id=1, source_target_pairs={{1008,0},{0,16},{16,32},{32,48},{48,64},{64,80},{80,96},{96,112},{... | collective-permute-start | bytes 196616 | tf_op jit(solution)/shard_map/while/body/eval_jaxpr/ppermute | solution.py:12
  230.9 5.6 %collective-permute-start.1 = (bf16[128,256]{0,1:T(8,128)(2,1)S(1)}, bf16[128,256]{0,1:T(8,128)(2,1)S(1)}, u32[]{:S(2)}, u32[]{:S(2)}) collective-permute-start(bf16[128,256]{0,1:T(8,128)(2,1)S(1)} %get-tuple-element.374), channel_id=1, source_target_pairs={{1008,0},{0,16},{16,32},{32,48},{48,64},{64,80},{80,96},{96,112},{... | collective-permute-start | bytes 196616 | tf_op jit(solution)/shard_map/while/body/eval_jaxpr/ppermute | solution.py:12
  236.8 5.6 %collective-permute-start.1 = (bf16[128,256]{0,1:T(8,128)(2,1)S(1)}, bf16[128,256]{0,1:T(8,128)(2,1)S(1)}, u32[]{:S(2)}, u32[]{:S(2)}) collective-permute-start(bf16[128,256]{0,1:T(8,128)(2,1)S(1)} %get-tuple-element.374), channel_id=1, source_target_pairs={{1008,0},{0,16},{16,32},{32,48},{48,64},{64,80},{80,96},{96,112},{... | collective-permute-start | bytes 196616 | tf_op jit(solution)/shard_map/while/body/eval_jaxpr/ppermute | solution.py:12
  242.7 5.6 %collective-permute-start.1 = (bf16[128,256]{0,1:T(8,128)(2,1)S(1)}, bf16[128,256]{0,1:T(8,128)(2,1)S(1)}, u32[]{:S(2)}, u32[]{:S(2)}) collective-permute-start(bf16[128,256]{0,1:T(8,128)(2,1)S(1)} %get-tuple-element.374), channel_id=1, source_target_pairs={{1008,0},{0,16},{16,32},{32,48},{48,64},{64,80},{80,96},{96,112},{... | collective-permute-start | bytes 196616 | tf_op jit(solution)/shard_map/while/body/eval_jaxpr/ppermute | solution.py:12
  248.6 5.6 %collective-permute-start.1 = (bf16[128,256]{0,1:T(8,128)(2,1)S(1)}, bf16[128,256]{0,1:T(8,128)(2,1)S(1)}, u32[]{:S(2)}, u32[]{:S(2)}) collective-permute-start(bf16[128,256]{0,1:T(8,128)(2,1)S(1)} %get-tuple-element.374), channel_id=1, source_target_pairs={{1008,0},{0,16},{16,32},{32,48},{48,64},{64,80},{80,96},{96,112},{... | collective-permute-start | bytes 196616 | tf_op jit(solution)/shard_map/while/body/eval_jaxpr/ppermute | solution.py:12
  254.5 5.6 %collective-permute-start.1 = (bf16[128,256]{0,1:T(8,128)(2,1)S(1)}, bf16[128,256]{0,1:T(8,128)(2,1)S(1)}, u32[]{:S(2)}, u32[]{:S(2)}) collective-permute-start(bf16[128,256]{0,1:T(8,128)(2,1)S(1)} %get-tuple-element.374), channel_id=1, source_target_pairs={{1008,0},{0,16},{16,32},{32,48},{48,64},{64,80},{80,96},{96,112},{... | collective-permute-start | bytes 196616 | tf_op jit(solution)/shard_map/while/body/eval_jaxpr/ppermute | solution.py:12
  260.5 5.6 %collective-permute-start.1 = (bf16[128,256]{0,1:T(8,128)(2,1)S(1)}, bf16[128,256]{0,1:T(8,128)(2,1)S(1)}, u32[]{:S(2)}, u32[]{:S(2)}) collective-permute-start(bf16[128,256]{0,1:T(8,128)(2,1)S(1)} %get-tuple-element.374), channel_id=1, source_target_pairs={{1008,0},{0,16},{16,32},{32,48},{48,64},{64,80},{80,96},{96,112},{... | collective-permute-start | bytes 196616 | tf_op jit(solution)/shard_map/while/body/eval_jaxpr/ppermute | solution.py:12
  266.4 5.6 %collective-permute-start.1 = (bf16[128,256]{0,1:T(8,128)(2,1)S(1)}, bf16[128,256]{0,1:T(8,128)(2,1)S(1)}, u32[]{:S(2)}, u32[]{:S(2)}) collective-permute-start(bf16[128,256]{0,1:T(8,128)(2,1)S(1)} %get-tuple-element.374), channel_id=1, source_target_pairs={{1008,0},{0,16},{16,32},{32,48},{48,64},{64,80},{80,96},{96,112},{... | collective-permute-start | bytes 196616 | tf_op jit(solution)/shard_map/while/body/eval_jaxpr/ppermute | solution.py:12
  272.3 5.6 %collective-permute-start.1 = (bf16[128,256]{0,1:T(8,128)(2,1)S(1)}, bf16[128,256]{0,1:T(8,128)(2,1)S(1)}, u32[]{:S(2)}, u32[]{:S(2)}) collective-permute-start(bf16[128,256]{0,1:T(8,128)(2,1)S(1)} %get-tuple-element.374), channel_id=1, source_target_pairs={{1008,0},{0,16},{16,32},{32,48},{48,64},{64,80},{80,96},{96,112},{... | collective-permute-start | bytes 196616 | tf_op jit(solution)/shard_map/while/body/eval_jaxpr/ppermute | solution.py:12
  278.2 5.6 %collective-permute-start.1 = (bf16[128,256]{0,1:T(8,128)(2,1)S(1)}, bf16[128,256]{0,1:T(8,128)(2,1)S(1)}, u32[]{:S(2)}, u32[]{:S(2)}) collective-permute-start(bf16[128,256]{0,1:T(8,128)(2,1)S(1)} %get-tuple-element.374), channel_id=1, source_target_pairs={{1008,0},{0,16},{16,32},{32,48},{48,64},{64,80},{80,96},{96,112},{... | collective-permute-start | bytes 196616 | tf_op jit(solution)/shard_map/while/body/eval_jaxpr/ppermute | solution.py:12
  284.1 5.6 %collective-permute-start.1 = (bf16[128,256]{0,1:T(8,128)(2,1)S(1)}, bf16[128,256]{0,1:T(8,128)(2,1)S(1)}, u32[]{:S(2)}, u32[]{:S(2)}) collective-permute-start(bf16[128,256]{0,1:T(8,128)(2,1)S(1)} %get-tuple-element.374), channel_id=1, source_target_pairs={{1008,0},{0,16},{16,32},{32,48},{48,64},{64,80},{80,96},{96,112},{... | collective-permute-start | bytes 196616 | tf_op jit(solution)/shard_map/while/body/eval_jaxpr/ppermute | solution.py:12
  290.0 5.6 %collective-permute-start.1 = (bf16[128,256]{0,1:T(8,128)(2,1)S(1)}, bf16[128,256]{0,1:T(8,128)(2,1)S(1)}, u32[]{:S(2)}, u32[]{:S(2)}) collective-permute-start(bf16[128,256]{0,1:T(8,128)(2,1)S(1)} %get-tuple-element.374), channel_id=1, source_target_pairs={{1008,0},{0,16},{16,32},{32,48},{48,64},{64,80},{80,96},{96,112},{... | collective-permute-start | bytes 196616 | tf_op jit(solution)/shard_map/while/body/eval_jaxpr/ppermute | solution.py:12
  295.9 5.6 %collective-permute-start.1 = (bf16[128,256]{0,1:T(8,128)(2,1)S(1)}, bf16[128,256]{0,1:T(8,128)(2,1)S(1)}, u32[]{:S(2)}, u32[]{:S(2)}) collective-permute-start(bf16[128,256]{0,1:T(8,128)(2,1)S(1)} %get-tuple-element.374), channel_id=1, source_target_pairs={{1008,0},{0,16},{16,32},{32,48},{48,64},{64,80},{80,96},{96,112},{... | collective-permute-start | bytes 196616 | tf_op jit(solution)/shard_map/while/body/eval_jaxpr/ppermute | solution.py:12
  301.8 5.6 %collective-permute-start.1 = (bf16[128,256]{0,1:T(8,128)(2,1)S(1)}, bf16[128,256]{0,1:T(8,128)(2,1)S(1)}, u32[]{:S(2)}, u32[]{:S(2)}) collective-permute-start(bf16[128,256]{0,1:T(8,128)(2,1)S(1)} %get-tuple-element.374), channel_id=1, source_target_pairs={{1008,0},{0,16},{16,32},{32,48},{48,64},{64,80},{80,96},{96,112},{... | collective-permute-start | bytes 196616 | tf_op jit(solution)/shard_map/while/body/eval_jaxpr/ppermute | solution.py:12
  307.7 5.6 %collective-permute-start.1 = (bf16[128,256]{0,1:T(8,128)(2,1)S(1)}, bf16[128,256]{0,1:T(8,128)(2,1)S(1)}, u32[]{:S(2)}, u32[]{:S(2)}) collective-permute-start(bf16[128,256]{0,1:T(8,128)(2,1)S(1)} %get-tuple-element.374), channel_id=1, source_target_pairs={{1008,0},{0,16},{16,32},{32,48},{48,64},{64,80},{80,96},{96,112},{... | collective-permute-start | bytes 196616 | tf_op jit(solution)/shard_map/while/body/eval_jaxpr/ppermute | solution.py:12
  313.6 5.6 %collective-permute-start.1 = (bf16[128,256]{0,1:T(8,128)(2,1)S(1)}, bf16[128,256]{0,1:T(8,128)(2,1)S(1)}, u32[]{:S(2)}, u32[]{:S(2)}) collective-permute-start(bf16[128,256]{0,1:T(8,128)(2,1)S(1)} %get-tuple-element.374), channel_id=1, source_target_pairs={{1008,0},{0,16},{16,32},{32,48},{48,64},{64,80},{80,96},{96,112},{... | collective-permute-start | bytes 196616 | tf_op jit(solution)/shard_map/while/body/eval_jaxpr/ppermute | solution.py:12
  319.5 5.6 %collective-permute-start.1 = (bf16[128,256]{0,1:T(8,128)(2,1)S(1)}, bf16[128,256]{0,1:T(8,128)(2,1)S(1)}, u32[]{:S(2)}, u32[]{:S(2)}) collective-permute-start(bf16[128,256]{0,1:T(8,128)(2,1)S(1)} %get-tuple-element.374), channel_id=1, source_target_pairs={{1008,0},{0,16},{16,32},{32,48},{48,64},{64,80},{80,96},{96,112},{... | collective-permute-start | bytes 196616 | tf_op jit(solution)/shard_map/while/body/eval_jaxpr/ppermute | solution.py:12
  325.4 5.6 %collective-permute-start.1 = (bf16[128,256]{0,1:T(8,128)(2,1)S(1)}, bf16[128,256]{0,1:T(8,128)(2,1)S(1)}, u32[]{:S(2)}, u32[]{:S(2)}) collective-permute-start(bf16[128,256]{0,1:T(8,128)(2,1)S(1)} %get-tuple-element.374), channel_id=1, source_target_pairs={{1008,0},{0,16},{16,32},{32,48},{48,64},{64,80},{80,96},{96,112},{... | collective-permute-start | bytes 196616 | tf_op jit(solution)/shard_map/while/body/eval_jaxpr/ppermute | solution.py:12
  331.3 5.6 %collective-permute-start.1 = (bf16[128,256]{0,1:T(8,128)(2,1)S(1)}, bf16[128,256]{0,1:T(8,128)(2,1)S(1)}, u32[]{:S(2)}, u32[]{:S(2)}) collective-permute-start(bf16[128,256]{0,1:T(8,128)(2,1)S(1)} %get-tuple-element.374), channel_id=1, source_target_pairs={{1008,0},{0,16},{16,32},{32,48},{48,64},{64,80},{80,96},{96,112},{... | collective-permute-start | bytes 196616 | tf_op jit(solution)/shard_map/while/body/eval_jaxpr/ppermute | solution.py:12
  337.2 5.6 %collective-permute-start.1 = (bf16[128,256]{0,1:T(8,128)(2,1)S(1)}, bf16[128,256]{0,1:T(8,128)(2,1)S(1)}, u32[]{:S(2)}, u32[]{:S(2)}) collective-permute-start(bf16[128,256]{0,1:T(8,128)(2,1)S(1)} %get-tuple-element.374), channel_id=1, source_target_pairs={{1008,0},{0,16},{16,32},{32,48},{48,64},{64,80},{80,96},{96,112},{... | collective-permute-start | bytes 196616 | tf_op jit(solution)/shard_map/while/body/eval_jaxpr/ppermute | solution.py:12
  343.1 5.6 %collective-permute-start.1 = (bf16[128,256]{0,1:T(8,128)(2,1)S(1)}, bf16[128,256]{0,1:T(8,128)(2,1)S(1)}, u32[]{:S(2)}, u32[]{:S(2)}) collective-permute-start(bf16[128,256]{0,1:T(8,128)(2,1)S(1)} %get-tuple-element.374), channel_id=1, source_target_pairs={{1008,0},{0,16},{16,32},{32,48},{48,64},{64,80},{80,96},{96,112},{... | collective-permute-start | bytes 196616 | tf_op jit(solution)/shard_map/while/body/eval_jaxpr/ppermute | solution.py:12
  349.0 5.6 %collective-permute-start.1 = (bf16[128,256]{0,1:T(8,128)(2,1)S(1)}, bf16[128,256]{0,1:T(8,128)(2,1)S(1)}, u32[]{:S(2)}, u32[]{:S(2)}) collective-permute-start(bf16[128,256]{0,1:T(8,128)(2,1)S(1)} %get-tuple-element.374), channel_id=1, source_target_pairs={{1008,0},{0,16},{16,32},{32,48},{48,64},{64,80},{80,96},{96,112},{... | collective-permute-start | bytes 196616 | tf_op jit(solution)/shard_map/while/body/eval_jaxpr/ppermute | solution.py:12
  354.9 5.6 %collective-permute-start.1 = (bf16[128,256]{0,1:T(8,128)(2,1)S(1)}, bf16[128,256]{0,1:T(8,128)(2,1)S(1)}, u32[]{:S(2)}, u32[]{:S(2)}) collective-permute-start(bf16[128,256]{0,1:T(8,128)(2,1)S(1)} %get-tuple-element.374), channel_id=1, source_target_pairs={{1008,0},{0,16},{16,32},{32,48},{48,64},{64,80},{80,96},{96,112},{... | collective-permute-start | bytes 196616 | tf_op jit(solution)/shard_map/while/body/eval_jaxpr/ppermute | solution.py:12
  360.9 5.6 %collective-permute-start.1 = (bf16[128,256]{0,1:T(8,128)(2,1)S(1)}, bf16[128,256]{0,1:T(8,128)(2,1)S(1)}, u32[]{:S(2)}, u32[]{:S(2)}) collective-permute-start(bf16[128,256]{0,1:T(8,128)(2,1)S(1)} %get-tuple-element.374), channel_id=1, source_target_pairs={{1008,0},{0,16},{16,32},{32,48},{48,64},{64,80},{80,96},{96,112},{... | collective-permute-start | bytes 196616 | tf_op jit(solution)/shard_map/while/body/eval_jaxpr/ppermute | solution.py:12
  372.7 5.6 %collective-permute-start.1 = (bf16[128,256]{0,1:T(8,128)(2,1)S(1)}, bf16[128,256]{0,1:T(8,128)(2,1)S(1)}, u32[]{:S(2)}, u32[]{:S(2)}) collective-permute-start(bf16[128,256]{0,1:T(8,128)(2,1)S(1)} %get-tuple-element.374), channel_id=1, source_target_pairs={{1008,0},{0,16},{16,32},{32,48},{48,64},{64,80},{80,96},{96,112},{... | collective-permute-start | bytes 196616 | tf_op jit(solution)/shard_map/while/body/eval_jaxpr/ppermute | solution.py:12
  378.6 5.6 %collective-permute-start.1 = (bf16[128,256]{0,1:T(8,128)(2,1)S(1)}, bf16[128,256]{0,1:T(8,128)(2,1)S(1)}, u32[]{:S(2)}, u32[]{:S(2)}) collective-permute-start(bf16[128,256]{0,1:T(8,128)(2,1)S(1)} %get-tuple-element.374), channel_id=1, source_target_pairs={{1008,0},{0,16},{16,32},{32,48},{48,64},{64,80},{80,96},{96,112},{... | collective-permute-start | bytes 196616 | tf_op jit(solution)/shard_map/while/body/eval_jaxpr/ppermute | solution.py:12
  390.4 5.6 %collective-permute-start.1 = (bf16[128,256]{0,1:T(8,128)(2,1)S(1)}, bf16[128,256]{0,1:T(8,128)(2,1)S(1)}, u32[]{:S(2)}, u32[]{:S(2)}) collective-permute-start(bf16[128,256]{0,1:T(8,128)(2,1)S(1)} %get-tuple-element.374), channel_id=1, source_target_pairs={{1008,0},{0,16},{16,32},{32,48},{48,64},{64,80},{80,96},{96,112},{... | collective-permute-start | bytes 196616 | tf_op jit(solution)/shard_map/while/body/eval_jaxpr/ppermute | solution.py:12
  (66 other events, 342.6 us)
where the time goes:
time: 400 us; the launch traced here: 397 us
  waiting for transfers between devices  217 us (54%)
  loops' own time  86.4 us (22%)
  local copies, waits for them, and re-layouts  44.2 us (11%)
  matrix products  30.5 us (8%)
  starting transfers between devices  13.7 us (3%)
  other arithmetic  5.2 us (1%)
    ppermute x126, waiting for transfers between devices, shifted(): return lax.ppermute(block, axis, route)  213 us
    another operation x1, loops' own time, body(): lax.fori_loop(1, seq_count, cycle_turn, ((keys, values), state))  86.4 us
    dynamic_slice x63, local copies, waits for them, and re-layouts, absorb(): visible = block_order[source % seq_count] < mine  41 us
    dot_general x64, matrix products, tile(): jnp.einsum('hqk,khd->qhd', weight.astype(jnp.bfloat16), v_three, preferre...  15.7 us
    dot_general x64, matrix products, tile(): jnp.einsum('qhd,khd->hqk', q_three, k_three, preferred_element_type=jnp.f...  14.8 us
  transfers between devices with their start and end apart: 127, of which 64 were waited for; matrix products, arithmetic and copies ran while one was open for 15% of the time, Pallas kernels for 0%

commit v1 on v0

v1 whole, which is shorter than its diff:
```python
import functools
import math

import jax
import jax.numpy as jnp
from jax import lax
from jax.experimental import pallas as pl
from jax.experimental.pallas import tpu as pltpu
from jax.sharding import PartitionSpec as P

D = 128
MESH = pl.DeviceIdType.MESH
NEG = -1e30
SPLIT = 2
COMPUTE = True


def kernel(
    nz, ny, nx,
    order_ref, q_ref, k_ref, v_ref, out_ref,
    buf, qx, qy, qf, qt, m_ref, l_ref, acc_ref, ost, osend,
    ring_sem, sent_sem, part_sem, own_sem, qx_sem, qy_sem, qf_sem, q_sent, o_sem,
):
    seq = lax.axis_index("seq")
    head = lax.axis_index("head")
    z, c = seq // 2, seq % 2
    y, x = head // nx, head % nx
    half = nz // 2
    rows = D // SPLIT
    other = 1 - c

    up = (2 * ((z + 1) % nz) + c, head)
    down = (2 * ((z + nz - 1) % nz) + c, head)
    toward = (up, down)
    partner = (2 * z + other, head)
    along_x = [(seq, y * nx + (x + i) % nx) for i in range(1, nx)]
    along_y = [(seq, ((y + i) % ny) * nx + x) for i in range(1, ny)]

    barrier = pltpu.get_barrier_semaphore()
    peers = [up, down, partner] + along_x + along_y
    for peer in peers:
        pl.semaphore_signal(barrier, inc=1, device_id=peer, device_id_type=MESH)
    pl.semaphore_wait(barrier, len(peers))

    def slot(d, t, kv, j):
        return ((d * (half + 1) + t) * 2 + kv) * 2 + j

    def piece_sem(d, t, kv, j, r):
        return slot(d, t, kv, j) * SPLIT + r

    def cols(which):
        return pl.ds(pl.multiple_of(which * D, D), D)

    def send(src, d, t, kv, j, r):
        pltpu.make_async_remote_copy(
            src_ref=src,
            dst_ref=buf.at[slot(d, t, kv, j), pl.ds(r * rows, rows)],
            send_sem=sent_sem.at[d],
            recv_sem=ring_sem.at[piece_sem(d, t, kv, j, r)],
            device_id=toward[d],
            device_id_type=MESH,
        ).start()

    def arrived(d, t, kv, j, r):
        ref = buf.at[slot(d, t, kv, j), pl.ds(r * rows, rows)]
        pltpu.make_async_copy(ref, ref, ring_sem.at[piece_sem(d, t, kv, j, r)]).wait()

    for kv, ref in enumerate((k_ref, v_ref)):
        for r in range(SPLIT):
            for d in range(2):
                send(ref.at[pl.ds(r * rows, rows), cols(c)], d, 1, kv, c, r)
        pltpu.make_async_remote_copy(
            src_ref=ref.at[:, cols(other)],
            dst_ref=buf.at[slot(0, 0, kv, c)],
            send_sem=own_sem.at[0],
            recv_sem=part_sem.at[kv],
            device_id=partner,
            device_id_type=MESH,
        ).start()
        pltpu.make_async_copy(
            ref.at[:, cols(c)], buf.at[slot(0, 0, kv, c)], own_sem.at[1]
        ).start()

    for i, peer in enumerate(along_x):
        to_x = (x + i + 1) % nx
        for b in range(ny):
            pltpu.make_async_remote_copy(
                src_ref=q_ref.at[:, pl.ds(pl.multiple_of((b * nx + to_x) * 2 * D, D), 2 * D)],
                dst_ref=qx.at[b, x],
                send_sem=q_sent.at[0],
                recv_sem=qx_sem.at[i],
                device_id=peer,
                device_id_type=MESH,
            ).start()
    for b in range(ny):
        pltpu.make_async_copy(
            q_ref.at[:, pl.ds(pl.multiple_of((b * nx + x) * 2 * D, D), 2 * D)],
            qx.at[b, x],
            q_sent.at[1],
        ).start()

    for kv in range(2):
        ref = buf.at[slot(0, 0, kv, other)]
        pltpu.make_async_copy(ref, ref, part_sem.at[kv]).wait()
        for r in range(SPLIT):
            for d in range(2):
                send(buf.at[slot(0, 0, kv, other), pl.ds(r * rows, rows)], d, 1, kv, other, r)

    def ring_step(t):
        for turn in range(2):
            j = (c + turn) % 2
            for kv in range(2):
                for r in range(SPLIT):
                    for d in range(2):
                        arrived(d, t, kv, j, r)
                        send(buf.at[slot(d, t, kv, j), pl.ds(r * rows, rows)], d, t + 1, kv, j, r)

    def queries_along_y():
        blocks = qx.at[:, 0]
        for i in range(nx - 1):
            pltpu.make_async_copy(blocks, blocks, qx_sem.at[i]).wait()
        pltpu.make_async_copy(blocks, blocks, q_sent.at[1]).wait()
        for i, peer in enumerate(along_y):
            pltpu.make_async_remote_copy(
                src_ref=qx.at[(y + i + 1) % ny],
                dst_ref=qy.at[y],
                send_sem=q_sent.at[2],
                recv_sem=qy_sem.at[i],
                device_id=peer,
                device_id_type=MESH,
            ).start()
        pltpu.make_async_copy(qx.at[y], qy.at[y], q_sent.at[3]).start()

    def queries_to_partner():
        for i in range(ny - 1):
            pltpu.make_async_copy(qy.at[0], qy.at[0], qy_sem.at[i]).wait()
        pltpu.make_async_copy(qy.at[0], qy.at[0], q_sent.at[3]).wait()
        pltpu.make_async_remote_copy(
            src_ref=qy.at[:, :, :, cols(other)],
            dst_ref=qf.at[c],
            send_sem=q_sent.at[4],
            recv_sem=qf_sem,
            device_id=partner,
            device_id_type=MESH,
        ).start()
        pltpu.make_async_copy(qy.at[:, :, :, cols(c)], qf.at[c], q_sent.at[5]).start()

    def queries_ready():
        pltpu.make_async_copy(qf.at[0], qf.at[0], qf_sem).wait()
        pltpu.make_async_copy(qf.at[0], qf.at[0], q_sent.at[5]).wait()
        for j in range(2):
            block = qf[j].astype(jnp.float32).reshape(D, D)
            qt[:, j * D:(j + 1) * D] = block.T.astype(jnp.bfloat16)

    lane = lax.broadcasted_iota(jnp.int32, (1, 2 * D), 1)
    q_order = jnp.where(lane < D, order_ref[2 * z], order_ref[2 * z + 1])
    factor = math.log2(math.e) / math.sqrt(D)

    def scores(k):
        return jnp.dot(k, qt[...], preferred_element_type=jnp.float32)

    def mix(v, weight):
        return lax.dot_general(
            v, weight.astype(jnp.bfloat16), (((0,), (0,)), ((), ())),
            preferred_element_type=jnp.float32,
        )

    def diagonal():
        for kv in range(2):
            ref = buf.at[slot(0, 0, kv, c)]
            pltpu.make_async_copy(ref, ref, own_sem.at[1]).wait()
        k = buf[slot(0, 0, 0, 0):slot(0, 0, 0, 0) + 2].reshape(2 * D, D)
        v = buf[slot(0, 0, 1, 0):slot(0, 0, 1, 0) + 2].reshape(2 * D, D)
        key = lax.broadcasted_iota(jnp.int32, (2 * D, 2 * D), 0)
        query = lax.broadcasted_iota(jnp.int32, (2 * D, 2 * D), 1)
        key_pos = jnp.where(key < D, order_ref[2 * z] * D, order_ref[2 * z + 1] * D - D) + key
        query_pos = jnp.where(query < D, order_ref[2 * z] * D, order_ref[2 * z + 1] * D - D) + query
        s = jnp.where(key_pos <= query_pos, scores(k) * factor, NEG)
        top = jnp.max(s, axis=0, keepdims=True)
        weight = jnp.exp2(s - top)
        m_ref[...] = top
        l_ref[...] = jnp.sum(weight, axis=0, keepdims=True)
        acc_ref[...] = mix(v, weight)

    def attend(sources):
        old = m_ref[...]
        new = old
        parts = []
        for key_slot, value_slot, count, block in sources:
            s = scores(buf[pl.ds(key_slot, count)].reshape(count * D, D))
            for j in range(count):
                seen = order_ref[block + j] < q_order
                part = s[j * D:(j + 1) * D] * factor
                top = jnp.max(part, axis=0, keepdims=True)
                new = jnp.maximum(new, jnp.where(seen, top, NEG))
                parts.append((part, seen))
        total = jnp.zeros_like(new)
        mixed = None
        at = 0
        for key_slot, value_slot, count, block in sources:
            weights = []
            for j in range(count):
                part, seen = parts[at]
                at += 1
                weight = jnp.exp2(part - jnp.where(seen, new, -NEG))
                total = total + jnp.sum(weight, axis=0, keepdims=True)
                weights.append(weight)
            got = mix(buf[pl.ds(value_slot, count)].reshape(count * D, D), jnp.concatenate(weights, axis=0))
            mixed = got if mixed is None else mixed + got
        scale = jnp.exp2(old - new)
        m_ref[...] = new
        l_ref[...] = l_ref[...] * scale + total
        acc_ref[...] = acc_ref[...] * scale + mixed

    def attend_step(t):
        attend([
            (slot(0, t, 0, 0), slot(0, t, 1, 0), 2, 2 * ((z - t + nz) % nz)),
            (slot(1, t, 0, 0), slot(1, t, 1, 0), 2, 2 * ((z + t) % nz)),
        ])

    ring_step(1)
    queries_along_y()
    ring_step(2)
    queries_to_partner()
    ring_step(3)
    queries_ready()
    if COMPUTE:
        diagonal()

    def two_steps(t, _):
        ring_step(t)

        def one(u, _):
            if COMPUTE:
                attend_step(u)
            return 0

        lax.fori_loop(2 * t - 7, 2 * t - 5, one, 0)
        return 0

    lax.fori_loop(4, 6, two_steps, 0)

    def one_step(t, _):
        ring_step(t)
        if COMPUTE:
            attend_step(t - 1)
        return 0

    lax.fori_loop(6, half - 1, one_step, 0)

    for d in range(2):
        for kv in range(2):
            for r in range(SPLIT):
                arrived(d, half - 1, kv, d, r)
                send(buf.at[slot(d, half - 1, kv, d), pl.ds(r * rows, rows)], d, half, kv, d, r)
    if COMPUTE:
        attend_step(half - 2)
    for d in range(2):
        for kv in range(2):
            for r in range(SPLIT):
                arrived(d, half - 1, kv, 1 - d, r)
    if COMPUTE:
        attend_step(half - 1)
    for d in range(2):
        for kv in range(2):
            for r in range(SPLIT):
                arrived(d, half, kv, d, r)
    far = 2 * ((z + half) % nz)
    if COMPUTE:
        attend([
            (slot(0, half, 0, 0), slot(0, half, 1, 0), 1, far),
            (slot(1, half, 0, 1), slot(1, half, 1, 1), 1, far + 1),
        ])
    result = acc_ref[...] / l_ref[...]
    first = jnp.transpose(result[:, :D]).astype(jnp.bfloat16)
    second = jnp.transpose(result[:, D:]).astype(jnp.bfloat16)
    osend[...] = jnp.where(c == 0, second, first)
    give = pltpu.make_async_remote_copy(
        src_ref=osend,
        dst_ref=ost.at[:, cols(c)],
        send_sem=o_sem.at[0],
        recv_sem=o_sem.at[1],
        device_id=partner,
        device_id_type=MESH,
    )
    give.start()
    ost[:, cols(c)] = jnp.where(c == 0, first, second)

    count = 2 * (2 * half - 1)
    for d in range(2):
        ref = buf.at[pl.ds(0, count)]
        pltpu.make_async_copy(ref, ref, sent_sem.at[d]).wait()
    ref = buf.at[pl.ds(0, 2)]
    pltpu.make_async_copy(ref, ref, own_sem.at[0]).wait()
    ref = qx.at[pl.ds(0, nx - 1)]
    pltpu.make_async_copy(ref, ref, q_sent.at[0]).wait()
    ref = qy.at[pl.ds(0, ny - 1)]
    pltpu.make_async_copy(ref, ref, q_sent.at[2]).wait()
    pltpu.make_async_copy(qf.at[0], qf.at[0], q_sent.at[4]).wait()
    give.wait()
    done = pltpu.make_async_copy(ost, out_ref, o_sem.at[2])
    done.start()
    done.wait()


def body(nz, ny, nx, queries, keys, values, block_order):
    half = nz // 2
    blocks = 2 * (half + 1) * 2 * 2
    any_space = pl.BlockSpec(memory_space=pl.ANY)
    bf16, f32 = jnp.bfloat16, jnp.float32
    return pl.pallas_call(
        functools.partial(kernel, nz, ny, nx),
        out_shape=jax.ShapeDtypeStruct((D, 2 * D), bf16),
        in_specs=[pl.BlockSpec(memory_space=pltpu.SMEM), any_space, any_space, any_space],
        out_specs=any_space,
        scratch_shapes=[
            pltpu.VMEM((blocks, D, D), bf16),
            pltpu.VMEM((ny, nx, 8, 2 * D), bf16),
            pltpu.VMEM((ny, nx, 8, 2 * D), bf16),
            pltpu.VMEM((2, ny, nx, 8, D), bf16),
            pltpu.VMEM((D, 2 * D), bf16),
            pltpu.VMEM((1, 2 * D), f32),
            pltpu.VMEM((1, 2 * D), f32),
            pltpu.VMEM((D, 2 * D), f32),
            pltpu.VMEM((D, 2 * D), bf16),
            pltpu.VMEM((D, D), bf16),
            pltpu.SemaphoreType.DMA((blocks * SPLIT,)),
            pltpu.SemaphoreType.DMA((2,)),
            pltpu.SemaphoreType.DMA((2,)),
            pltpu.SemaphoreType.DMA((2,)),
            pltpu.SemaphoreType.DMA((nx - 1,)),
            pltpu.SemaphoreType.DMA((ny - 1,)),
            pltpu.SemaphoreType.DMA,
            pltpu.SemaphoreType.DMA((6,)),
            pltpu.SemaphoreType.DMA((3,)),
        ],
        compiler_params=pltpu.CompilerParams(
            collective_id=0, has_side_effects=True, vmem_limit_bytes=32 << 20
        ),
    )(block_order, queries, keys, values)


def solution(mesh):
    nz, ny, nx = mesh.shape["seq"] // 2, 4, mesh.shape["head"] // 4
    in_specs = (P(("seq", "head"), None), P("seq", "head"), P("seq", "head"), P())
    return jax.shard_map(
        functools.partial(body, nz, ny, nx),
        mesh=mesh, in_specs=in_specs, out_specs=P("seq", "head"), check_vma=False,
    )
```

time: 400 us -> 82.7 us (0.21)
  waiting for transfers between devices: 217 us -> 0 us
  loops' own time: 86.4 us -> 0 us
  Pallas kernels: 0 us -> 78.6 us
  local copies, waits for them, and re-layouts: 44.2 us -> 3.8 us
  matrix products: 30.5 us -> 0 us
  starting transfers between devices: 13.7 us -> 0 us
  other arithmetic: 5.2 us -> 0 us
    ppermute x126 -> x0, waiting for transfers between devices: 213 us -> none  [shifted(): return lax.ppermute(block, axis, route)]
    another operation x1 -> x0, loops' own time: 86.4 us -> none  [body(): lax.fori_loop(1, seq_count, cycle_turn, ((keys, values), state))]
    pallas_call x0 -> x1, Pallas kernels: none -> 78.6 us  [body(): pl.pallas_call(functools.partial(kernel, nz, ny, nx), out_shape=jax.Shape...]
    dynamic_slice x64 -> x0, local copies, waits for them, and re-layouts: 41.6 us -> none  [the longest x63 41 us: absorb(): visible = block_order[source % seq_count] < mine]
    dot_general x128 -> x0, matrix products: 30.5 us -> none  [the longest x64 15.7 us: tile(): jnp.einsum('hqk,khd->qhd', weight.astype(jnp.bfloat16), v_three, preferre...]
    all_to_all x1 -> x0, starting transfers between devices: 7.7 us -> none  [body(): lax.all_to_all(queries, 'head', split_axis=1, concat_axis=0, tiled=True)]
    ppermute x126 -> x0, starting transfers between devices: 5.96 us -> none  [shifted(): return lax.ppermute(block, axis, route)]
    all_to_all x1 -> x0, waiting for transfers between devices: 4.25 us -> none  [body(): lax.all_to_all(queries, 'head', split_axis=1, concat_axis=0, tiled=True)]
  transfers between devices with their start and end apart: 127 -> 0, of which waited for: 64 -> 0; matrix products, arithmetic and copies ran while one was open for 15% -> 0% of each run, Pallas kernels for 0% -> 0%
where the time goes in v1:
time: 82.7 us; the launch traced here: 82.4 us
  Pallas kernels  78.6 us (95%)
  local copies, waits for them, and re-layouts  3.8 us (5%)
    pallas_call x1, Pallas kernels, body(): pl.pallas_call(functools.partial(kernel, nz, ny, nx), out_shape=jax.Shape...  78.6 us
    unnamed x9, local copies, waits for them, and re-layouts  3.8 us

profile of v1, /device:TPU:1, one launch (start us, length us, event | category | flops | bytes accessed | tf_op | source)
XLA Modules:
  0.0 82.4 jit_solution(6418920240737346634)
XLA Ops:
  0.0 0.0 copy-start
  0.0 0.8 %copy-done = bf16[8,4096]{1,0:T(8,128)(2,1)S(1)} copy-done((bf16[8,4096]{1,0:T(8,128)(2,1)S(1)}, bf16[8,4096]{1,0:T(8,128)(2,1)}, u32[]{:S(2)}) %copy-start) | copy-done | bytes 65560
  0.8 0.0 copy-start.1
  0.8 0.8 %copy-done.1 = bf16[128,256]{1,0:T(8,128)(2,1)S(1)} copy-done((bf16[128,256]{1,0:T(8,128)(2,1)S(1)}, bf16[128,256]{1,0:T(8,128)(2,1)}, u32[]{:S(2)}) %copy-start.1) | copy-done | bytes 65560
  1.7 0.0 copy-start.2
  1.7 0.8 %copy-done.2 = bf16[128,256]{1,0:T(8,128)(2,1)S(1)} copy-done((bf16[128,256]{1,0:T(8,128)(2,1)S(1)}, bf16[128,256]{1,0:T(8,128)(2,1)}, u32[]{:S(2)}) %copy-start.2) | copy-done | bytes 65560
  2.5 0.0 copy-start.3
  2.5 0.7 copy-done.3
  3.2 78.6 %shard_map.46 = bf16[128,256]{1,0:T(8,128)(2,1)S(1)} custom-call(s32[64]{0:T(128)S(1)} %copy-done.3, bf16[8,4096]{1,0:T(8,128)(2,1)S(1)} %copy-done, bf16[128,256]{1,0:T(8,128)(2,1)S(1)} %copy-done.1, bf16[128,256]{1,0:T(8,128)(2,1)S(1)} %copy-done.2), custom_call_target="tpu_custom_call" | custom-call | tf_op jit(solution)/shard_map/pallas_call | solution.py:311
  81.8 0.6 copy.6
Async XLA Ops:
  0.0 0.8 %copy-start = (bf16[8,4096]{1,0:T(8,128)(2,1)S(1)}, bf16[8,4096]{1,0:T(8,128)(2,1)}, u32[]{:S(2)}) copy-start(bf16[8,4096]{1,0:T(8,128)(2,1)} %q_ref.1) | copy-start | bytes 196612
  0.8 0.8 %copy-start.1 = (bf16[128,256]{1,0:T(8,128)(2,1)S(1)}, bf16[128,256]{1,0:T(8,128)(2,1)}, u32[]{:S(2)}) copy-start(bf16[128,256]{1,0:T(8,128)(2,1)} %k_ref.1) | copy-start | bytes 196612
  1.7 0.8 %copy-start.2 = (bf16[128,256]{1,0:T(8,128)(2,1)S(1)}, bf16[128,256]{1,0:T(8,128)(2,1)}, u32[]{:S(2)}) copy-start(bf16[128,256]{1,0:T(8,128)(2,1)} %v_ref.1) | copy-start | bytes 196612
  2.5 0.7 copy-start.3
